TPU v7x, 256 devices: a whole 4x4x8 slice. The times are simulated.
256 devices in a mesh: ctx: 8 (over x, core), tp: 32 (over y, z).
Axes of the slice: x: 4, y: 4, z: 8, core: 2. Of those that a mesh axis runs over, the one named last changes fastest.
Arguments:
- tokens: bfloat16 [1024, 8192], P('ctx', 'tp'), may hold values from -6 to 6
- in_weight: bfloat16 [8192, 3, 8192], P(None, None, 'tp'), may hold values from -0.0625 to 0.0625
- filter_taps: float32 [3, 3, 8192], P(None, None, 'tp'), may hold values from -2.4 to 2.4
- decay_rate: float32 [16, 8192], P(None, 'tp'), may hold values from 0.0001953125 to 0.08, as said below
- residue: float32 [16, 8192], P(None, 'tp'), may hold values from -80 to 80
Outputs:
- gated: bfloat16 [1024, 8192], P('ctx', 'tp')
Inputs may be any that keep to these rules, and one draw needn't show every extreme that they name: `decay_rate`: every decay rate lies between 0.2 / 1024 and 0.08.
All inputs are finite; a program needn't handle non-finite values.
Results may differ from a plain program's by a relative error of at most 0.015.
Values may be sent and summed in bfloat16 or wider, within the bound.
A program may use at most 128 MiB of HBM per device.

v0:
```python
import jax
import jax.numpy as jnp
from jax import lax
from jax.sharding import PartitionSpec as P

BLOCK = 128


def passed_along(value, axis, steps):
    count = lax.axis_size(axis)
    first, last = (max(0, -steps), min(count, count - steps))
    return lax.ppermute(value, axis, [(source, source + steps) for source in range(first, last)])


def entering(value, axis, join, neutral):
    count, mine = (lax.axis_size(axis), lax.axis_index(axis))
    pieces = jax.tree.map(lambda part: lax.all_gather(part, axis), value)
    total = jax.tree.map(
        lambda part, zero: jnp.full_like(part, 0) + jnp.asarray(zero, part.dtype), value, neutral
    )

    def step(position, total):
        longer = join(total, jax.tree.map(lambda part: part[position], pieces))
        return jax.tree.map(lambda new, old: jnp.where(position < mine, new, old), longer, total)

    return lax.fori_loop(0, count - 1, step, total)


def project(row_block, in_weight):
    weight_flat = in_weight.reshape(in_weight.shape[0], -1)
    gathered = lax.all_gather(row_block, "tp", axis=1, tiled=True)
    summed = jnp.dot(gathered, weight_flat, preferred_element_type=jnp.float32)
    return summed.astype(jnp.bfloat16).reshape(row_block.shape[0], 3, -1)


def combine_modes(earlier, later):
    return (earlier[0] * later[0], later[0] * earlier[1] + later[1])


def on_device(tokens, in_weight, filter_taps, decay_rate, residue):
    row_count = tokens.shape[0]
    lead_rows = filter_taps.shape[0] - 1
    projected = project(tokens, in_weight)
    rim_rows = passed_along(projected[row_count - lead_rows :], "ctx", 1)
    padded = jnp.concatenate([rim_rows, projected], axis=0)
    features = jnp.zeros((row_count,) + padded.shape[1:], jnp.float32)
    for lag_index in range(lead_rows + 1):
        window = padded[lead_rows - lag_index : lead_rows - lag_index + row_count].astype(
            jnp.float32
        )
        features = features + filter_taps[lag_index] * window
    query_part = features[:, 0]
    source = features[:, 1] * features[:, 2]
    chan_count = source.shape[1]
    block_count = row_count // BLOCK
    coeffs = residue * jnp.sqrt(1.0 - jnp.exp(-2.0 * decay_rate))
    offsets = jnp.arange(BLOCK, dtype=jnp.float32)
    falling = jnp.exp(-decay_rate[None] * offsets[:, None, None])
    rising = jnp.exp(decay_rate[None] * offsets[:, None, None])
    toeplitz = jnp.einsum(
        "inc,jnc->ijc", falling * coeffs[None], rising, precision=lax.Precision.HIGHEST
    )
    lower_mask = (offsets[:, None] >= offsets[None, :])[:, :, None]
    toeplitz = jnp.where(lower_mask, toeplitz, 0.0)
    blocks = source.reshape(block_count, BLOCK, chan_count)
    inner_part = jnp.einsum("ijc,bjc->bic", toeplitz, blocks, precision=lax.Precision.HIGHEST)
    end_weights = falling[::-1]
    partial_states = jnp.einsum(
        "jnc,bjc->bnc", end_weights, blocks, precision=lax.Precision.HIGHEST
    )
    block_decay = jnp.exp(-decay_rate * BLOCK)

    def advance(carry_state, block_term):
        return (block_decay * carry_state + block_term, carry_state)

    local_end, local_starts = lax.scan(advance, jnp.zeros_like(block_decay), partial_states)
    device_decay = jnp.exp(-decay_rate * row_count)
    identity = (jnp.ones_like(local_end), jnp.zeros_like(local_end))
    prefix = entering((device_decay, local_end), "ctx", combine_modes, identity)
    incoming = prefix[1]
    start_offsets = jnp.arange(block_count, dtype=jnp.float32) * BLOCK
    start_states = (
        local_starts + jnp.exp(-decay_rate[None] * start_offsets[:, None, None]) * incoming[None]
    )
    read_weights = coeffs[None] * jnp.exp(-decay_rate[None] * (offsets + 1.0)[:, None, None])
    carried = jnp.einsum(
        "inc,bnc->bic", read_weights, start_states, precision=lax.Precision.HIGHEST
    )
    response = (inner_part + carried).reshape(row_count, chan_count)
    return (query_part * response).astype(jnp.bfloat16)


def solution(mesh):
    return jax.shard_map(
        on_device,
        mesh=mesh,
        in_specs=(
            P("ctx", "tp"),
            P(None, None, "tp"),
            P(None, None, "tp"),
            P(None, "tp"),
            P(None, "tp"),
        ),
        out_specs=P("ctx", "tp"),
        check_vma=False,
    )
```

profile of v0, /device:TPU:1, one launch (start us, length us, event | category | flops | bytes accessed | tf_op | source)
XLA Modules:
  0.0 242.4 jit_solution(11823663511975442552)
XLA Ops:
  6.5 0.0 all-gather.4.cloned.1.call-start
  6.5 0.7 all-gather.4.cloned.1.call-update
  7.3 0.0 copy-start
  7.3 0.0 copy-start.2
  7.3 16.7 %copy.9 = bf16[8192,3,256]{0,2,1:T(8,128)(2,1)} copy(bf16[8192,3,256]{2,0,1:T(8,128)(2,1)} %param.8) | data formatting | bytes 25165824 | tf_op args[1]
  24.0 0.0 copy-done
  24.0 0.0 copy-done.2
  24.0 1.6 multiply_exponential_fusion.1
  25.6 1.6 multiply_exponential_fusion
  27.2 58.1 %all-gather.4.cloned.1.call-done = bf16[128,8192]{1,0:T(8,128)(2,1)} async-done(((bf16[128,256]{1,0:T(8,128)(2,1)}), bf16[128,8192]{1,0:T(8,128)(2,1)}) %all-gather.4.cloned.1.call-update) | async-done | bytes 2097168 | tf_op jit(solution)/shard_map/all_gather | solution.py:31
  85.4 9.5 %convolution_convert_fusion = bf16[128,768]{1,0:T(8,128)(2,1)S(1)} fusion(bf16[128,8192]{1,0:T(8,128)(2,1)} %all-gather.4.cloned.1.call-done, bf16[8192,768]{0,1:T(8,128)(2,1)} %bitcast.64), kind=kOutput, calls=%fused_computation.8 | convolution fusion | flops 1610711040 | bytes 14876672 | tf_op jit(solution)/shard_map/dot_general | solution.py:32
  94.9 0.2 copy.32
  95.1 6.6 %collective-permute-start = (bf16[2,3,256]{0,2,1:T(8,128)(2,1)S(1)}, bf16[2,3,256]{0,2,1:T(8,128)(2,1)S(1)}, u32[]{:S(2)}, u32[]{:S(2)}) collective-permute-start(bf16[2,3,256]{0,2,1:T(8,128)(2,1)S(1)} %bitcast.70), channel_id=1, source_target_pairs={{0,32},{32,64},{64,96},{96,128},{128,160},{160,192},{192,224},{1,3... | collective-permute-start | bytes 9224 | tf_op jit(solution)/shard_map/ppermute | solution.py:12
  101.7 2.5 %copy.13 = f32[128,16,256]{0,1,2:T(8,128)S(1)} copy(f32[128,16,256]{2,1,0:T(8,128)} %multiply_exponential_fusion.1) | data formatting | bytes 4194304 | tf_op jit(solution)/shard_map/exp | solution.py:59
  104.3 0.2 copy.10
  104.4 0.0 collective-permute-done
  104.4 0.5 multiply_add_fusion
  105.0 0.0 copy-start.1
  105.0 0.1 copy.33
  105.1 1.8 multiply_reduce_fusion.1
  107.0 14.2 %all-gather = f32[128,256]{1,0:T(8,128)S(1)} all-gather(f32[16,256]{1,0:T(8,128)S(1)} %get-tuple-element.146), channel_id=2, replica_groups=mesh['ctx'=8,'tp'=32] {'ctx'}, dimensions={0}, use_global_device_ids=true | all-gather | bytes 147456 | tf_op jit(solution)/shard_map/all_gather | solution.py:17
  121.1 12.9 %all-gather.1 = f32[128,256]{1,0:T(8,128)S(1)} all-gather(f32[16,256]{1,0:T(8,128)S(1)} %get-tuple-element.145), channel_id=3, replica_groups=mesh['ctx'=8,'tp'=32] {'ctx'}, dimensions={0}, use_global_device_ids=true | all-gather | bytes 147456 | tf_op jit(solution)/shard_map/all_gather | solution.py:17
  134.1 0.3 while.9
  134.3 0.0 copy-done.1
  134.4 1.6 broadcast_multiply_fusion
  136.0 0.7 multiply_reduce_fusion
  136.7 0.1 copy.31
  136.8 3.4 %copy.14 = f32[128,16,256]{0,1,2:T(8,128)} copy(f32[128,16,256]{2,1,0:T(8,128)} %broadcast_multiply_fusion) | data formatting | bytes 4194304 | tf_op jit(solution)/shard_map/mul | solution.py:61
  140.1 29.8 %fusion.4 = f32[256,128,128]{2,1,0:T(8,128)} fusion(f32[128,16,256]{0,1,2:T(8,128)S(1)} %copy.13, f32[128,16,256]{0,1,2:T(8,128)} %copy.14), kind=kOutput, calls=%fused_computation.28 | convolution fusion | flops 805306368 | bytes 20971520 | tf_op jit(solution)/shard_map/inc,jnc->ijc/dot_general | solution.py:60
  169.9 17.8 %copy.15 = f32[256,128,128]{0,1,2:T(8,128)} copy(f32[256,128,128]{2,1,0:T(8,128)} %fusion.4) | data formatting | bytes 33554432 | tf_op jit(solution)/shard_map/inc,jnc->ijc/dot_general | solution.py:60
  187.7 12.2 %bitcast_select_fusion = f32[128,128,256]{2,1,0:T(8,128)} fusion(f32[256,128,128]{0,1,2:T(8,128)} %copy.15, pred[128,128]{1,0:T(8,128)(4,1)S(1)} %iota_compare_fusion), kind=kLoop, calls=%fused_computation.3 | loop fusion | flops 4194304 | bytes 33570816 | tf_op jit(solution)/shard_map/jit(_where)/select_n | solution.py:64
  199.9 18.3 %copy.17 = f32[128,128,256]{0,1,2:T(8,128)} copy(f32[128,128,256]{2,1,0:T(8,128)} %bitcast_select_fusion) | data formatting | bytes 33554432 | tf_op jit(solution)/shard_map/jit(_where)/select_n | solution.py:64
  218.2 16.6 %fusion.5 = f32[256,1,128]{2,1,0:T(1,128)S(1)} fusion(f32[128,256,1]{0,2,1:T(1,128)S(1)} %bitcast.66, f32[128,128,256]{0,1,2:T(8,128)} %copy.17), kind=kOutput, calls=%fused_computation.29 | convolution fusion | flops 50331648 | bytes 17039360 | tf_op jit(solution)/shard_map/ijc,bjc->bic/dot_general | solution.py:66
  234.8 0.7 copy.12
  (18 shorter events, 0.2 us)
Async XLA Ops:
  6.5 78.8 %all-gather.4.cloned.1.call-start = ((), (), s32[]{:S(2)}) async-start(), calls=%async_computation | async-start | bytes 2162688 | tf_op jit(solution)/shard_map/all_gather | solution.py:31
  7.3 16.7 %copy-start = (f32[16,256]{1,0:T(8,128)S(1)}, f32[16,256]{1,0:T(8,128)}, u32[]{:S(2)}) copy-start(f32[16,256]{1,0:T(8,128)} %param.10) | copy-start | bytes 49156
  7.3 16.7 %copy-start.2 = (f32[3,3,256]{2,1,0:T(4,128)S(1)}, f32[3,3,256]{2,1,0:T(4,128)}, u32[]{:S(2)}) copy-start(f32[3,3,256]{2,1,0:T(4,128)} %param.9) | copy-start | bytes 27652
  95.1 9.4 %collective-permute-start = (bf16[2,3,256]{0,2,1:T(8,128)(2,1)S(1)}, bf16[2,3,256]{0,2,1:T(8,128)(2,1)S(1)}, u32[]{:S(2)}, u32[]{:S(2)}) collective-permute-start(bf16[2,3,256]{0,2,1:T(8,128)(2,1)S(1)} %bitcast.70), channel_id=1, source_target_pairs={{0,32},{32,64},{64,96},{96,128},{128,160},{160,192},{192,224},{1,3... | collective-permute-start | bytes 9224 | tf_op jit(solution)/shard_map/ppermute | solution.py:12
  105.0 29.3 %copy-start.1 = (f32[16,256]{1,0:T(8,128)S(1)}, f32[16,256]{1,0:T(8,128)}, u32[]{:S(2)}) copy-start(f32[16,256]{1,0:T(8,128)} %param.11) | copy-start | bytes 49156
Sparse Core Ops, SparseCore 0:
  9.8 75.4 all-gather.3
where the time goes:
time: 243 us; the launch traced here: 242 us
  local copies, waits for them, and re-layouts  60 us (25%)
  waiting for transfers between devices  58.8 us (24%)
  matrix products  55.8 us (23%)
  blocking collectives  27.1 us (11%)
  other arithmetic  20.3 us (8%)
  between operations  13.6 us (6%)
  starting transfers between devices  6.64 us (3%)
    all_gather x1, waiting for transfers between devices, project(): gathered = lax.all_gather(row_block, 'tp', axis=1, tiled=True)  58.1 us
    dot_general x1, matrix products, on_device(): jnp.einsum('inc,jnc->ijc', falling * coeffs[None], rising, precision=lax....  29.8 us
    all_gather x2, blocking collectives, entering(): pieces = jax.tree.map(lambda part: lax.all_gather(part, axis), value)  27.1 us
    select_n x1, local copies, waits for them, and re-layouts, on_device(): toeplitz = jnp.where(lower_mask, toeplitz, 0.0)  18.3 us
    dot_general x1, local copies, waits for them, and re-layouts, on_device(): jnp.einsum('inc,jnc->ijc', falling * coeffs[None], rising, precision=lax....  17.8 us
    unnamed x8, local copies, waits for them, and re-layouts  16.8 us
    dot_general x1, matrix products, on_device(): jnp.einsum('ijc,bjc->bic', toeplitz, blocks, precision=lax.Precision.HIGH...  16.6 us
    select_n x1, other arithmetic, on_device(): toeplitz = jnp.where(lower_mask, toeplitz, 0.0)  12.2 us
  transfers between devices with their start and end apart: 2, of which 1 were waited for; matrix products, arithmetic and copies ran while one was open for 9% of the time, Pallas kernels for 0%

commit v1 on v0

--- a/solution.py
+++ b/solution.py
@@ -28,7 +28,13 @@
 
 def project(row_block, in_weight):
     weight_flat = in_weight.reshape(in_weight.shape[0], -1)
-    gathered = lax.all_gather(row_block, "tp", axis=1, tiled=True)
+
+    def part_masks(unit, named_axis):
+        return jnp.concatenate(
+            lax.all_to_all(jnp.stack(lax.psum(1, named_axis) * [unit]), named_axis, 0, 0), axis=1
+        )
+
+    gathered = part_masks(row_block, named_axis="tp")
     summed = jnp.dot(gathered, weight_flat, preferred_element_type=jnp.float32)
     return summed.astype(jnp.bfloat16).reshape(row_block.shape[0], 3, -1)
 

time: 243 us -> 213 us (0.88)
  waiting for transfers between devices: 58.8 us -> 28.9 us
  between operations: 13.6 us -> 0.21 us
  starting transfers between devices: 6.64 us -> 17.1 us
  local copies, waits for them, and re-layouts: 60 us -> 62.8 us
    all_gather x1 -> x0, waiting for transfers between devices: 58.1 us -> none  [project(): gathered = lax.all_gather(row_block, 'tp', axis=1, tiled=True)]
    all_to_all x0 -> x1, waiting for transfers between devices: none -> 28.9 us  [part_masks(): lax.all_to_all(jnp.stack(lax.psum(1, named_axis) * [unit]), named_axis, 0...]
    all_to_all x0 -> x1, starting transfers between devices: none -> 12 us  [part_masks(): lax.all_to_all(jnp.stack(lax.psum(1, named_axis) * [unit]), named_axis, 0...]
    unnamed x8 -> x9, local copies, waits for them, and re-layouts: 16.8 us -> 17.8 us
  transfers between devices with their start and end apart: 2 -> 2, of which waited for: 1 -> 1; matrix products, arithmetic and copies ran while one was open for 9% -> 11% of each run, Pallas kernels for 0% -> 0%
where the time goes in v1:
time: 213 us; the launch traced here: 212 us
  local copies, waits for them, and re-layouts  62.8 us (29%)
  matrix products  55.2 us (26%)
  waiting for transfers between devices  28.9 us (14%)
  blocking collectives  27.1 us (13%)
  other arithmetic  20.3 us (10%)
  starting transfers between devices  17.1 us (8%)
    dot_general x1, matrix products, on_device(): jnp.einsum('inc,jnc->ijc', falling * coeffs[None], rising, precision=lax....  29.8 us
    all_to_all x1, waiting for transfers between devices, part_masks(): lax.all_to_all(jnp.stack(lax.psum(1, named_axis) * [unit]), named_axis, 0...  28.9 us
    all_gather x2, blocking collectives, entering(): pieces = jax.tree.map(lambda part: lax.all_gather(part, axis), value)  27.1 us
    select_n x1, local copies, waits for them, and re-layouts, on_device(): toeplitz = jnp.where(lower_mask, toeplitz, 0.0)  18.3 us
    unnamed x9, local copies, waits for them, and re-layouts  17.8 us
    dot_general x1, local copies, waits for them, and re-layouts, on_device(): jnp.einsum('inc,jnc->ijc', falling * coeffs[None], rising, precision=lax....  17.8 us
    dot_general x1, matrix products, on_device(): jnp.einsum('ijc,bjc->bic', toeplitz, blocks, precision=lax.Precision.HIGH...  16.6 us
    select_n x1, other arithmetic, on_device(): toeplitz = jnp.where(lower_mask, toeplitz, 0.0)  12.2 us
  transfers between devices with their start and end apart: 2, of which 1 were waited for; matrix products, arithmetic and copies ran while one was open for 11% of the time, Pallas kernels for 0%

profile of v1, /device:TPU:1, one launch (start us, length us, event | category | flops | bytes accessed | tf_op | source)
XLA Modules:
  0.0 211.8 jit_solution(13360768212696764891)
XLA Ops:
  0.0 0.9 copy.9
  1.0 1.8 stack.2
  2.8 12.0 %all-to-all-start = ((bf16[32,128,256]{1,2,0:T(8,128)(2,1)}), bf16[32,128,256]{1,2,0:T(8,128)(2,1)S(1)}, u32[]{:S(2)}, u32[]{:S(2)}) async-start(bf16[32,128,256]{1,2,0:T(8,128)(2,1)} %stack.2), calls=%async_computation | async-start | bytes 4194304 | tf_op jit(solution)/shard_map/all_to_all | solution.py:34
  14.8 0.0 copy-start
  14.8 0.0 copy-start.2
  14.8 16.7 %copy.10 = bf16[8192,3,256]{0,2,1:T(8,128)(2,1)} copy(bf16[8192,3,256]{2,0,1:T(8,128)(2,1)} %param.8) | data formatting | bytes 25165824 | tf_op args[1]
  31.6 0.0 copy-done
  31.6 0.0 copy-done.2
  31.6 1.6 multiply_exponential_fusion.1
  33.2 1.6 multiply_exponential_fusion
  34.8 28.9 %all-to-all-done = bf16[32,128,256]{1,2,0:T(8,128)(2,1)S(1)} async-done(((bf16[32,128,256]{1,2,0:T(8,128)(2,1)}), bf16[32,128,256]{1,2,0:T(8,128)(2,1)S(1)}, u32[]{:S(2)}, u32[]{:S(2)}) %all-to-all-start) | async-done | bytes 2097184 | tf_op jit(solution)/shard_map/all_to_all | solution.py:34
  63.7 8.9 %convolution_convert_fusion = bf16[128,768]{1,0:T(8,128)(2,1)S(1)} fusion(bf16[128,8192]{0,1:T(8,128)(2,1)S(1)} %bitcast.68, bf16[8192,768]{0,1:T(8,128)(2,1)} %bitcast.67), kind=kOutput, calls=%fused_computation.8 | convolution fusion | flops 1610711040 | bytes 14876672 | tf_op jit(solution)/shard_map/dot_general | solution.py:38
  72.6 0.2 copy.33
  72.8 5.1 %collective-permute-start = (bf16[2,3,256]{0,2,1:T(8,128)(2,1)S(1)}, bf16[2,3,256]{0,2,1:T(8,128)(2,1)S(1)}, u32[]{:S(2)}, u32[]{:S(2)}) collective-permute-start(bf16[2,3,256]{0,2,1:T(8,128)(2,1)S(1)} %bitcast.74), channel_id=1, source_target_pairs={{0,32},{32,64},{64,96},{96,128},{128,160},{160,192},{192,224},{1,3... | collective-permute-start | bytes 9224 | tf_op jit(solution)/shard_map/ppermute | solution.py:12
  78.0 2.5 %copy.14 = f32[128,16,256]{0,1,2:T(8,128)S(1)} copy(f32[128,16,256]{2,1,0:T(8,128)} %multiply_exponential_fusion.1) | data formatting | bytes 4194304 | tf_op jit(solution)/shard_map/exp | solution.py:65
  80.5 0.2 copy.11
  80.6 0.0 collective-permute-done
  80.7 0.5 multiply_add_fusion
  81.2 0.0 copy-start.1
  81.2 0.1 copy.34
  81.4 1.8 multiply_reduce_fusion.1
  83.2 14.2 %all-gather = f32[128,256]{1,0:T(8,128)S(1)} all-gather(f32[16,256]{1,0:T(8,128)S(1)} %get-tuple-element.146), channel_id=2, replica_groups=mesh['ctx'=8,'tp'=32] {'ctx'}, dimensions={0}, use_global_device_ids=true | all-gather | bytes 147456 | tf_op jit(solution)/shard_map/all_gather | solution.py:17
  97.4 12.9 %all-gather.1 = f32[128,256]{1,0:T(8,128)S(1)} all-gather(f32[16,256]{1,0:T(8,128)S(1)} %get-tuple-element.145), channel_id=3, replica_groups=mesh['ctx'=8,'tp'=32] {'ctx'}, dimensions={0}, use_global_device_ids=true | all-gather | bytes 147456 | tf_op jit(solution)/shard_map/all_gather | solution.py:17
  110.3 0.3 while.9
  110.6 0.0 copy-done.1
  110.6 1.6 broadcast_multiply_fusion
  112.2 0.7 multiply_reduce_fusion
  112.9 0.1 copy.32
  113.0 3.4 %copy.15 = f32[128,16,256]{0,1,2:T(8,128)} copy(f32[128,16,256]{2,1,0:T(8,128)} %broadcast_multiply_fusion) | data formatting | bytes 4194304 | tf_op jit(solution)/shard_map/mul | solution.py:67
  116.3 29.8 %fusion.4 = f32[256,128,128]{2,1,0:T(8,128)} fusion(f32[128,16,256]{0,1,2:T(8,128)S(1)} %copy.14, f32[128,16,256]{0,1,2:T(8,128)} %copy.15), kind=kOutput, calls=%fused_computation.28 | convolution fusion | flops 805306368 | bytes 20971520 | tf_op jit(solution)/shard_map/inc,jnc->ijc/dot_general | solution.py:66
  146.1 17.8 %copy.16 = f32[256,128,128]{0,1,2:T(8,128)} copy(f32[256,128,128]{2,1,0:T(8,128)} %fusion.4) | data formatting | bytes 33554432 | tf_op jit(solution)/shard_map/inc,jnc->ijc/dot_general | solution.py:66
  163.9 12.2 %bitcast_select_fusion = f32[128,128,256]{2,1,0:T(8,128)} fusion(f32[256,128,128]{0,1,2:T(8,128)} %copy.16, pred[128,128]{1,0:T(8,128)(4,1)S(1)} %iota_compare_fusion), kind=kLoop, calls=%fused_computation.3 | loop fusion | flops 4194304 | bytes 33570816 | tf_op jit(solution)/shard_map/jit(_where)/select_n | solution.py:70
  176.1 18.3 %copy.18 = f32[128,128,256]{0,1,2:T(8,128)} copy(f32[128,128,256]{2,1,0:T(8,128)} %bitcast_select_fusion) | data formatting | bytes 33554432 | tf_op jit(solution)/shard_map/jit(_where)/select_n | solution.py:70
  194.4 16.6 %fusion.5 = f32[256,1,128]{2,1,0:T(1,128)S(1)} fusion(f32[128,256,1]{0,2,1:T(1,128)S(1)} %bitcast.70, f32[128,128,256]{0,1,2:T(8,128)} %copy.18), kind=kOutput, calls=%fused_computation.29 | convolution fusion | flops 50331648 | bytes 17039360 | tf_op jit(solution)/shard_map/ijc,bjc->bic/dot_general | solution.py:72
  211.0 0.7 copy.13
  (18 shorter events, 0.2 us)
Async XLA Ops:
  2.8 60.9 %all-to-all-start = ((bf16[32,128,256]{1,2,0:T(8,128)(2,1)}), bf16[32,128,256]{1,2,0:T(8,128)(2,1)S(1)}, u32[]{:S(2)}, u32[]{:S(2)}) async-start(bf16[32,128,256]{1,2,0:T(8,128)(2,1)} %stack.2), calls=%async_computation | async-start | bytes 4194304 | tf_op jit(solution)/shard_map/all_to_all | solution.py:34
  14.8 16.8 %copy-start = (f32[16,256]{1,0:T(8,128)S(1)}, f32[16,256]{1,0:T(8,128)}, u32[]{:S(2)}) copy-start(f32[16,256]{1,0:T(8,128)} %param.10) | copy-start | bytes 49156
  14.8 16.8 %copy-start.2 = (f32[3,3,256]{2,1,0:T(4,128)S(1)}, f32[3,3,256]{2,1,0:T(4,128)}, u32[]{:S(2)}) copy-start(f32[3,3,256]{2,1,0:T(4,128)} %param.9) | copy-start | bytes 27652
  72.8 7.8 %collective-permute-start = (bf16[2,3,256]{0,2,1:T(8,128)(2,1)S(1)}, bf16[2,3,256]{0,2,1:T(8,128)(2,1)S(1)}, u32[]{:S(2)}, u32[]{:S(2)}) collective-permute-start(bf16[2,3,256]{0,2,1:T(8,128)(2,1)S(1)} %bitcast.74), channel_id=1, source_target_pairs={{0,32},{32,64},{64,96},{96,128},{128,160},{160,192},{192,224},{1,3... | collective-permute-start | bytes 9224 | tf_op jit(solution)/shard_map/ppermute | solution.py:12
  81.2 29.4 %copy-start.1 = (f32[16,256]{1,0:T(8,128)S(1)}, f32[16,256]{1,0:T(8,128)}, u32[]{:S(2)}) copy-start(f32[16,256]{1,0:T(8,128)} %param.11) | copy-start | bytes 49156
